TPU v7x, 32 devices: a whole 2x2x4 slice. The times are simulated.
32 devices in a mesh: dp: 8 (over y, x, core), tensor: 4 (over z).
Axes of the slice: x: 2, y: 2, z: 4, core: 2. Of those that a mesh axis runs over, the one named last changes fastest.
Arguments:
- tokens: bfloat16 [6144, 2048], P(('dp', 'tensor')), may hold values from -6 to 6
- cotangent: bfloat16 [6144, 2048], P(('dp', 'tensor')), may hold values from -6 to 6
- deal: int32 [6144], P(('dp', 'tensor')), may hold values from 0 to 6143, as said below
- segment: int32 [6144], P('dp'), may hold values from 0 to 3, as said below
- norm1_gain: float32 [2, 2048], replicated, may hold values from 0.5 to 1.5
- norm1_shift: float32 [2, 2048], replicated, may hold values from -1.25 to 1.25
- query_weight: bfloat16 [2, 2048, 2048], P(None, 'dp', 'tensor'), may hold values from -0.125 to 0.125
- query_bias: float32 [2, 2048], P(None, 'tensor'), may hold values from -3 to 3
- kv_weight: bfloat16 [2, 2048, 256], P(None, 'dp', 'tensor'), may hold values from -0.125 to 0.125
- value_bias: float32 [2, 128], replicated, may hold values from -0.3125 to 0.3125
- out_weight: bfloat16 [2, 2048, 2048], P(None, 'tensor', 'dp'), may hold values from -1.5 to 1.5
- out_bias: float32 [2, 2048], replicated, may hold values from -1.75 to 1.75
- norm2_gain: float32 [2, 2048], replicated, may hold values from 0.5 to 1.5
- norm2_shift: float32 [2, 2048], replicated, may hold values from -1.25 to 1.25
- up_weight: bfloat16 [2, 2048, 8192], P(None, 'dp', 'tensor'), may hold values from -0.125 to 0.125
- up_bias: float32 [2, 8192], P(None, 'tensor'), may hold values from -3 to 3
- down_weight: bfloat16 [2, 8192, 2048], P(None, 'tensor', 'dp'), may hold values from -0.0625 to 0.0625
- down_bias: float32 [2, 2048], replicated, may hold values from -1.75 to 1.75
Outputs:
- layer_out: bfloat16 [6144, 2048], P(('dp', 'tensor'))
- tokens_grad: bfloat16 [6144, 2048], P(('dp', 'tensor'))
- norm1_gain_grad: float32 [2, 2048], replicated
- norm1_shift_grad: float32 [2, 2048], replicated
- query_weight_grad: float32 [2, 2048, 2048], P(None, 'dp', 'tensor')
- query_bias_grad: float32 [2, 2048], P(None, 'tensor')
- kv_weight_grad: float32 [2, 2048, 256], P(None, 'dp', 'tensor')
- value_bias_grad: float32 [2, 128], replicated
- out_weight_grad: float32 [2, 2048, 2048], P(None, 'tensor', 'dp')
- out_bias_grad: float32 [2, 2048], replicated
- norm2_gain_grad: float32 [2, 2048], replicated
- norm2_shift_grad: float32 [2, 2048], replicated
- up_weight_grad: float32 [2, 2048, 8192], P(None, 'dp', 'tensor')
- up_bias_grad: float32 [2, 8192], P(None, 'tensor')
- down_weight_grad: float32 [2, 8192, 2048], P(None, 'tensor', 'dp')
- down_bias_grad: float32 [2, 2048], replicated
Inputs may be any that keep to these rules, and one draw needn't show every extreme that they name: deal is a permutation: input row i becomes working row deal[i]; rows of both orders are laid out over the devices in order, 192 a device; a row stays on a device of the same tensor index, and every device deals exactly 24 rows to each dp index. `segment`: within each group of 768 working rows the labels never fall; each run of equal labels is one sequence of 96 to 768 rows; the first group is one sequence of all its rows.
All inputs are finite; a program needn't handle non-finite values.
Results may differ from a plain program's by a relative error of at most 0.025.
Values may be sent and summed in bfloat16 or wider, within the bound.
No kernel may reach another device: no remote copies, remote signals or barrier semaphores. Data moves between devices by JAX's collectives and lax.ppermute only.
A program may use at most 256 MiB of HBM per device.

v0:
```python
import jax
import jax.numpy as jnp
from jax import lax
from jax.sharding import PartitionSpec as P

HEAD = 128
EPSILON = 1e-05


def layer_norm(values, scales, offsets):
    row_mean = jnp.mean(values, axis=-1, keepdims=True)
    centred = values - row_mean
    row_var = jnp.mean(centred * centred, axis=-1, keepdims=True)
    return centred * lax.rsqrt(row_var + EPSILON) * scales + offsets


def gelu_tanh(values):
    return jax.nn.gelu(values, approximate=True)


def matmul(left, right):
    return jnp.dot(left, right, preferred_element_type=jnp.float32)


def contract_rows(left, right):
    return lax.dot_general(
        left, right, (((0,), (0,)), ((), ())), preferred_element_type=jnp.float32
    )


def contract_cols(left, right):
    return lax.dot_general(
        left, right, (((1,), (1,)), ((), ())), preferred_element_type=jnp.float32
    )


def rows_gather(values):
    return lax.all_gather(values, "tensor", axis=0, tiled=True)


def grad_gather(values):
    return lax.all_gather(values, "tensor", axis=0, tiled=True)


def rows_scatter(left, right):
    return lax.psum_scatter(
        matmul(left, right).astype(jnp.bfloat16), "tensor", scatter_dimension=0, tiled=True
    ).astype(jnp.float32)


def grad_scatter(factor_pairs):
    running = None
    for gradient, weight in factor_pairs:
        product_piece = contract_cols(gradient, weight)
        running = product_piece if running is None else running + product_piece
    return lax.psum_scatter(
        running.astype(jnp.bfloat16), "tensor", scatter_dimension=0, tiled=True
    ).astype(jnp.float32)


def place_slice(values, full_width, tensor_rank):
    start_col = tensor_rank * values.shape[0]
    return lax.dynamic_update_slice(jnp.zeros((full_width,), jnp.float32), values, (start_col,))


def local(
    tokens,
    cotangent,
    deal,
    segment,
    norm1_gain,
    norm1_shift,
    query_weight,
    query_bias,
    kv_weight,
    value_bias,
    out_weight,
    out_bias,
    norm2_gain,
    norm2_shift,
    up_weight,
    up_bias,
    down_weight,
    down_bias,
):
    local_rows = tokens.shape[0]
    dp_count = lax.axis_size("dp")
    tensor_count = lax.axis_size("tensor")
    tensor_rank = lax.axis_index("tensor")
    slot_rows = local_rows // dp_count
    layer_total = query_weight.shape[0]
    group_rows = local_rows * tensor_count
    query_cols = query_weight.shape[2]
    pair_width = kv_weight.shape[2]
    hidden_cols = up_weight.shape[2]
    head_count = query_cols // HEAD
    score_scale = HEAD ** (-0.5)
    target_dev = deal // local_rows // tensor_count
    target_row = deal % local_rows
    dev_ids = jnp.arange(dp_count, dtype=jnp.int32)
    dev_match = (target_dev[:, None] == dev_ids[None, :]).astype(jnp.int32)
    earlier = jnp.cumsum(dev_match, axis=0) - dev_match
    slot_of = target_dev * slot_rows + jnp.sum(earlier * dev_match, axis=1)
    row_ids = jnp.arange(local_rows, dtype=jnp.int32)
    send_mask = row_ids[:, None] == slot_of[None, :]
    send_table = send_mask.astype(jnp.bfloat16)
    sent_place = jnp.sum(jnp.where(send_mask, target_row[None, :], 0), axis=1)
    arrived_place = lax.all_to_all(sent_place, "dp", split_axis=0, concat_axis=0, tiled=True)
    tokens_sent = matmul(send_table, tokens).astype(jnp.bfloat16)
    tangent_sent = matmul(send_table, cotangent).astype(jnp.bfloat16)
    tokens_come, tangent_come = (
        lax.all_to_all(tokens_sent, "dp", split_axis=0, concat_axis=0, tiled=True),
        lax.all_to_all(tangent_sent, "dp", split_axis=0, concat_axis=0, tiled=True),
    )
    place_table = (row_ids[:, None] == arrived_place[None, :]).astype(jnp.bfloat16)
    stream = matmul(place_table, tokens_come)
    tangent = matmul(place_table, tangent_come)
    places = jnp.arange(group_rows, dtype=jnp.int32)
    allowed = (places[None, :] <= places[:, None]) & (segment[:, None] == segment[None, :])
    saved = []
    kept_weights = []
    for layer_index in range(layer_total):
        w_query, w_pair, w_out, w_up, w_down = (
            lax.all_gather(query_weight[layer_index], "dp", axis=0, tiled=True),
            lax.all_gather(kv_weight[layer_index], "dp", axis=0, tiled=True),
            lax.all_gather(out_weight[layer_index], "dp", axis=1, tiled=True),
            lax.all_gather(up_weight[layer_index], "dp", axis=0, tiled=True),
            lax.all_gather(down_weight[layer_index], "dp", axis=1, tiled=True),
        )
        kept_weights.append(None)
        normed_one = layer_norm(stream, norm1_gain[layer_index], norm1_shift[layer_index]).astype(
            jnp.bfloat16
        )
        normed_all = rows_gather(normed_one)
        queries = (matmul(normed_all, w_query) + query_bias[layer_index]).astype(jnp.bfloat16)
        full_bias = jnp.concatenate([jnp.zeros((HEAD,), jnp.float32), value_bias[layer_index]])
        pair_bias = lax.dynamic_slice_in_dim(full_bias, tensor_rank * pair_width, pair_width)
        pair_local = (matmul(normed_all, w_pair) + pair_bias).astype(jnp.bfloat16)
        pair_all = lax.all_gather(pair_local, "tensor", axis=1, tiled=True)
        key_rows = pair_all[:, :HEAD]
        value_rows = pair_all[:, HEAD:]
        query_heads = jnp.transpose(queries.reshape(group_rows, head_count, HEAD), (1, 0, 2))

        def attend(query_one):
            scores = jnp.where(allowed, contract_cols(query_one, key_rows) * score_scale, -1e30)
            row_top = jnp.max(scores, axis=-1, keepdims=True)
            exp_score = jnp.exp(scores - row_top)
            row_total = jnp.sum(exp_score, axis=-1, keepdims=True)
            weights = (exp_score / row_total).astype(jnp.bfloat16)
            return (matmul(weights, value_rows), (row_top + jnp.log(row_total))[:, 0])

        head_outs, log_totals = lax.map(attend, query_heads)
        mixed = (
            jnp.transpose(head_outs, (1, 0, 2)).reshape(group_rows, query_cols).astype(jnp.bfloat16)
        )
        hidden_state = stream + rows_scatter(mixed, w_out) + out_bias[layer_index]
        normed_two = layer_norm(
            hidden_state, norm2_gain[layer_index], norm2_shift[layer_index]
        ).astype(jnp.bfloat16)
        normed_two_all = rows_gather(normed_two)
        pre_gelu = matmul(normed_two_all, w_up) + up_bias[layer_index]
        activation = gelu_tanh(pre_gelu).astype(jnp.bfloat16)
        saved.append(
            (
                stream,
                normed_all,
                queries,
                pair_all,
                log_totals,
                mixed,
                hidden_state,
                normed_two_all,
                pre_gelu,
                activation,
            )
        )
        stream = hidden_state + rows_scatter(activation, w_down) + down_bias[layer_index]
    layer_out = stream.astype(jnp.bfloat16)
    reduced_by_layer = [None] * layer_total
    small_by_layer = [None] * layer_total
    for layer_index in reversed(range(layer_total)):
        (
            stream_in,
            normed_all,
            queries,
            pair_all,
            log_totals,
            mixed,
            hidden_state,
            normed_two_all,
            pre_gelu,
            activation,
        ) = saved[layer_index]
        w_query, w_pair, w_out, w_up, w_down = (
            lax.all_gather(query_weight[layer_index], "dp", axis=0, tiled=True),
            lax.all_gather(kv_weight[layer_index], "dp", axis=0, tiled=True),
            lax.all_gather(out_weight[layer_index], "dp", axis=1, tiled=True),
            lax.all_gather(up_weight[layer_index], "dp", axis=0, tiled=True),
            lax.all_gather(down_weight[layer_index], "dp", axis=1, tiled=True),
        )
        key_rows = pair_all[:, :HEAD]
        value_rows = pair_all[:, HEAD:]
        branch_grad = tangent.astype(jnp.bfloat16)
        down_bias_part = jnp.sum(branch_grad.astype(jnp.float32), axis=0)
        branch_all = grad_gather(branch_grad)
        down_grad = contract_rows(activation, branch_all)
        act_grad = contract_cols(branch_all, w_down)
        pre_grad = jax.vjp(gelu_tanh, pre_gelu)[1](act_grad)[0].astype(jnp.bfloat16)
        up_bias_part = jnp.sum(pre_grad.astype(jnp.float32), axis=0)
        up_grad = contract_rows(normed_two_all, pre_grad)
        normed_two_grad = grad_scatter(((pre_grad, w_up),))
        norm_pull_two = jax.vjp(
            layer_norm, hidden_state, norm2_gain[layer_index], norm2_shift[layer_index]
        )[1]
        hidden_part, gain_two_part, shift_two_part = norm_pull_two(normed_two_grad)
        hidden_grad = tangent + hidden_part
        attn_grad = hidden_grad.astype(jnp.bfloat16)
        out_bias_part = jnp.sum(attn_grad.astype(jnp.float32), axis=0)
        attn_all = grad_gather(attn_grad)
        out_grad = contract_rows(mixed, attn_all)
        mixed_grad = contract_cols(attn_all, w_out).astype(jnp.bfloat16)
        query_heads = jnp.transpose(queries.reshape(group_rows, head_count, HEAD), (1, 0, 2))
        dout_heads = jnp.transpose(mixed_grad.reshape(group_rows, head_count, HEAD), (1, 0, 2))

        def attend_back(carried, inputs):
            query_one, dout_one, log_one = inputs
            scores = jnp.where(allowed, contract_cols(query_one, key_rows) * score_scale, -1e30)
            probs = jnp.exp(scores - log_one[:, None])
            prob_grad = contract_cols(dout_one, value_rows)
            inner = jnp.sum(probs * prob_grad, axis=-1, keepdims=True)
            score_grad = (probs * (prob_grad - inner) * score_scale).astype(jnp.bfloat16)
            key_acc = carried[0] + contract_rows(score_grad, query_one)
            value_acc = carried[1] + contract_rows(probs.astype(jnp.bfloat16), dout_one)
            return ((key_acc, value_acc), matmul(score_grad, key_rows))

        start_acc = (
            jnp.zeros((group_rows, HEAD), jnp.float32),
            jnp.zeros((group_rows, HEAD), jnp.float32),
        )
        (key_grad, value_grad), query_grads = lax.scan(
            attend_back, start_acc, (query_heads, dout_heads, log_totals)
        )
        query_grad = (
            jnp.transpose(query_grads, (1, 0, 2))
            .reshape(group_rows, query_cols)
            .astype(jnp.bfloat16)
        )
        query_bias_part = jnp.sum(query_grad.astype(jnp.float32), axis=0)
        pair_part = jnp.concatenate([key_grad, value_grad], axis=1)
        pair_grad = lax.psum_scatter(
            pair_part.astype(jnp.bfloat16), "tensor", scatter_dimension=1, tiled=True
        )
        pair_bias_part = jnp.sum(pair_grad.astype(jnp.float32), axis=0)
        query_w_grad = contract_rows(normed_all, query_grad)
        pair_w_grad = contract_rows(normed_all, pair_grad)
        normed_grad = grad_scatter(((query_grad, w_query), (pair_grad, w_pair)))
        norm_pull_one = jax.vjp(
            layer_norm, stream_in, norm1_gain[layer_index], norm1_shift[layer_index]
        )[1]
        stream_part, gain_one_part, shift_one_part = norm_pull_one(normed_grad)
        tangent = hidden_grad + stream_part
        small_by_layer[layer_index] = (
            gain_one_part,
            shift_one_part,
            place_slice(query_bias_part, query_cols * tensor_count, tensor_rank),
            place_slice(pair_bias_part, pair_width * tensor_count, tensor_rank),
            out_bias_part,
            gain_two_part,
            shift_two_part,
            place_slice(up_bias_part, hidden_cols * tensor_count, tensor_rank),
            down_bias_part,
        )
        reduced_by_layer[layer_index] = (
            lax.psum_scatter(
                query_w_grad.astype(jnp.bfloat16), "dp", scatter_dimension=0, tiled=True
            ).astype(jnp.float32),
            lax.psum_scatter(
                pair_w_grad.astype(jnp.bfloat16), "dp", scatter_dimension=0, tiled=True
            ).astype(jnp.float32),
            lax.psum_scatter(
                out_grad.astype(jnp.bfloat16), "dp", scatter_dimension=1, tiled=True
            ).astype(jnp.float32),
            lax.psum_scatter(
                up_grad.astype(jnp.bfloat16), "dp", scatter_dimension=0, tiled=True
            ).astype(jnp.float32),
            lax.psum_scatter(
                down_grad.astype(jnp.bfloat16), "dp", scatter_dimension=1, tiled=True
            ).astype(jnp.float32),
        )
    summed = [
        jnp.stack([reduced_by_layer[layer_index][member] for layer_index in range(layer_total)])
        for member in range(5)
    ]
    smalls = [
        jnp.stack([small_by_layer[layer_index][member] for layer_index in range(layer_total)])
        for member in range(9)
    ]
    (
        gain_one_sum,
        shift_one_sum,
        query_bias_sum,
        pair_bias_sum,
        out_bias_sum,
        gain_two_sum,
        shift_two_sum,
        up_bias_sum,
        down_bias_sum,
    ) = lax.psum(
        (
            smalls[0],
            smalls[1],
            smalls[2],
            smalls[3],
            smalls[4],
            smalls[5],
            smalls[6],
            smalls[7],
            smalls[8],
        ),
        ("dp", "tensor"),
    )
    query_bias_grad = lax.dynamic_slice_in_dim(
        query_bias_sum, tensor_rank * query_cols, query_cols, 1
    )
    up_bias_grad = lax.dynamic_slice_in_dim(up_bias_sum, tensor_rank * hidden_cols, hidden_cols, 1)
    value_bias_grad = pair_bias_sum[:, HEAD:]
    out_slots = contract_rows(place_table, layer_out).astype(jnp.bfloat16)
    grad_slots = contract_rows(place_table, tangent.astype(jnp.bfloat16)).astype(jnp.bfloat16)
    out_back, grad_back = (
        lax.all_to_all(out_slots, "dp", split_axis=0, concat_axis=0, tiled=True),
        lax.all_to_all(grad_slots, "dp", split_axis=0, concat_axis=0, tiled=True),
    )
    layer_rows = contract_rows(send_table, out_back).astype(jnp.bfloat16)
    token_rows = contract_rows(send_table, grad_back).astype(jnp.bfloat16)
    return (
        layer_rows,
        token_rows,
        gain_one_sum,
        shift_one_sum,
        summed[0],
        query_bias_grad,
        summed[1],
        value_bias_grad,
        summed[2],
        out_bias_sum,
        gain_two_sum,
        shift_two_sum,
        summed[3],
        up_bias_grad,
        summed[4],
        down_bias_sum,
    )


def solution(mesh):
    in_specs = (
        P(("dp", "tensor"), None),
        P(("dp", "tensor"), None),
        P(("dp", "tensor")),
        P("dp"),
        P(),
        P(),
        P(None, "dp", "tensor"),
        P(None, "tensor"),
        P(None, "dp", "tensor"),
        P(),
        P(None, "tensor", "dp"),
        P(),
        P(),
        P(),
        P(None, "dp", "tensor"),
        P(None, "tensor"),
        P(None, "tensor", "dp"),
        P(),
    )
    out_specs = (
        P(("dp", "tensor"), None),
        P(("dp", "tensor"), None),
        P(),
        P(),
        P(None, "dp", "tensor"),
        P(None, "tensor"),
        P(None, "dp", "tensor"),
        P(),
        P(None, "tensor", "dp"),
        P(),
        P(),
        P(),
        P(None, "dp", "tensor"),
        P(None, "tensor"),
        P(None, "tensor", "dp"),
        P(),
    )
    return jax.shard_map(local, mesh=mesh, in_specs=in_specs, out_specs=out_specs, check_vma=False)
```

profile of v0, /device:TPU:0, one launch (start us, length us, event | category | flops | bytes accessed | tf_op | source)
XLA Modules:
  0.0 2494.6 jit_solution(4482688082752972419)
XLA Ops:
  9.8 5.2 all-to-all-start
  25.6 10.0 all-to-all-done.1
  41.3 8.8 all-gather.1
  50.9 50.5 %all-gather.27.cloned.1.call-done = bf16[768,2048]{1,0:T(8,128)(2,1)} async-done(((bf16[192,2048]{1,0:T(8,128)(2,1)}), bf16[768,2048]{1,0:T(8,128)(2,1)}) %all-gather.27.cloned.1.call-update) | async-done | bytes 3145744 | tf_op jit(solution)/shard_map/all_gather | solution.py:38
  104.3 15.1 all_gather.73
  119.7 10.7 all-gather.43.cloned.1.call-done
  135.8 34.1 %while.56 = (s32[]{:T(128)}, bf16[4,768,128]{1,2,0:T(8,128)(2,1)S(1)}, f32[4,768]{1,0:T(4,128)}, bf16[4,768,128]{2,1,0:T(8,128)(2,1)S(1)}, bf16[768,128]{1,0:T(8...) while((s32[]{:T(128)}, ...), condition=%wide.region_9.10_spmd.clone, body=%wide.region_6.9_spmd.clone.sunk | while | flops 308477184 | bytes 8108645 | solution.py:152
  170.0 5.7 convolution_convert_fusion.5
  179.2 56.9 %reduce-scatter.25.cloned.1.call-done = bf16[192,2048]{1,0:T(8,128)(2,1)} async-done(((bf16[768,2048]{1,0:T(8,128)(2,1)}), bf16[192,2048]{1,0:T(8,128)(2,1)}) %reduce-scatter.25.cloned.1.call-update) | async-done | bytes 786448 | tf_op jit(solution)/shard_map/reduce_scatter | solution.py:46
  242.8 50.0 %all-gather.47.cloned.1.call-done = bf16[1,2048,2048]{2,1,0:T(8,128)(2,1)} async-done(((bf16[1,256,2048]{2,1,0:T(8,128)(2,1)}), bf16[1,2048,2048]{2,1,0:T(8,128)(2,1)}) %all-gather.47.cloned.1.call-update) | async-done | bytes 8388624 | tf_op jit(solution)/shard_map/all_gather | solution.py:127
  292.9 65.5 %all-gather.29.cloned.1.call-done = bf16[768,2048]{1,0:T(8,128)(2,1)} async-done(((bf16[192,2048]{1,0:T(8,128)(2,1)}), bf16[768,2048]{1,0:T(8,128)(2,1)}) %all-gather.29.cloned.1.call-update) | async-done | bytes 3145744 | tf_op jit(solution)/shard_map/all_gather | solution.py:38
  358.4 11.7 fusion.66
  370.1 45.4 %all-gather.49.cloned.1.call-done = bf16[1,2048,2048]{2,1,0:T(8,128)(2,1)} async-done(((bf16[1,2048,256]{2,1,0:T(8,128)(2,1)}), bf16[1,2048,2048]{2,1,0:T(8,128)(2,1)}) %all-gather.49.cloned.1.call-update) | async-done | bytes 8388624 | tf_op jit(solution)/shard_map/all_gather | solution.py:128
  415.5 13.1 fusion.85
  430.0 59.0 %reduce-scatter.27.cloned.1.call-done = bf16[192,2048]{1,0:T(8,128)(2,1)} async-done(((bf16[768,2048]{1,0:T(8,128)(2,1)}), bf16[192,2048]{1,0:T(8,128)(2,1)}) %reduce-scatter.27.cloned.1.call-update) | async-done | bytes 786448 | tf_op jit(solution)/shard_map/reduce_scatter | solution.py:46
  493.0 11.0 all-gather.6
  504.0 14.9 all-gather.51.cloned.1.call-done
  518.9 65.5 %all-gather.31.cloned.1.call-done = bf16[768,2048]{1,0:T(8,128)(2,1)} async-done(((bf16[192,2048]{1,0:T(8,128)(2,1)}), bf16[768,2048]{1,0:T(8,128)(2,1)}) %all-gather.31.cloned.1.call-update) | async-done | bytes 3145744 | tf_op jit(solution)/shard_map/all_gather | solution.py:38
  584.4 5.3 add_convert_fusion.5
  594.3 15.1 all_gather.81
  611.0 33.6 %while.57 = (s32[]{:T(128)}, bf16[4,768,128]{1,2,0:T(8,128)(2,1)S(1)}, f32[4,768]{1,0:T(4,128)}, bf16[4,768,128]{2,1,0:T(8,128)(2,1)S(1)}, bf16[768,128]{1,0:T(8...) while((s32[]{:T(128)}, ...), condition=%wide.region_19.20_spmd.clone, body=%wide.region_16.19_spmd.clone.sunk | while | flops 308477184 | bytes 8108645 | solution.py:152
  644.7 5.7 convolution_convert_fusion.4
  651.2 57.8 %reduce-scatter.29.cloned.1.call-done = bf16[192,2048]{1,0:T(8,128)(2,1)} async-done(((bf16[768,2048]{1,0:T(8,128)(2,1)}), bf16[192,2048]{1,0:T(8,128)(2,1)}) %reduce-scatter.29.cloned.1.call-update) | async-done | bytes 786448 | tf_op jit(solution)/shard_map/reduce_scatter | solution.py:46
  712.6 22.7 all_to_all.57
  738.0 32.3 %all-gather.55.cloned.1.call-done = bf16[1,2048,2048]{2,1,0:T(8,128)(2,1)} async-done(((bf16[1,256,2048]{2,1,0:T(8,128)(2,1)}), bf16[1,2048,2048]{2,1,0:T(8,128)(2,1)}) %all-gather.55.cloned.1.call-update) | async-done | bytes 8388624 | tf_op jit(solution)/shard_map/all_gather | solution.py:127
  770.2 65.5 %all-gather.33.cloned.1.call-done = bf16[768,2048]{1,0:T(8,128)(2,1)} async-done(((bf16[192,2048]{1,0:T(8,128)(2,1)}), bf16[768,2048]{1,0:T(8,128)(2,1)}) %all-gather.33.cloned.1.call-update) | async-done | bytes 3145744 | tf_op jit(solution)/shard_map/all_gather | solution.py:38
  835.7 11.8 fusion.58
  847.5 52.4 %all-gather.35.cloned.1.call-done = bf16[768,2048]{1,0:T(8,128)(2,1)} async-done(((bf16[192,2048]{1,0:T(8,128)(2,1)}), bf16[768,2048]{1,0:T(8,128)(2,1)}) %all-gather.35.cloned.1.call-update) | async-done | bytes 3145744 | tf_op jit(solution)/shard_map/all_gather | solution.py:42
  899.9 56.9 %all-gather.57.cloned.1.call-done = bf16[1,2048,2048]{2,1,0:T(8,128)(2,1)} async-done(((bf16[1,2048,256]{2,1,0:T(8,128)(2,1)}), bf16[1,2048,2048]{2,1,0:T(8,128)(2,1)}) %all-gather.57.cloned.1.call-update) | async-done | bytes 8388624 | tf_op jit(solution)/shard_map/all_gather | solution.py:128
  956.9 15.4 convert_reduce_fusion
  973.9 8.1 fusion.88
  982.1 60.4 %reduce-scatter.33.cloned.1.call-done = bf16[192,2048]{1,0:T(8,128)(2,1)} async-done(((bf16[768,2048]{1,0:T(8,128)(2,1)}), bf16[192,2048]{1,0:T(8,128)(2,1)}) %reduce-scatter.33.cloned.1.call-update) | async-done | bytes 786448 | tf_op jit(solution)/shard_map/reduce_scatter | solution.py:56
  1047.8 63.4 %all-gather.37.cloned.1.call-done = bf16[768,2048]{1,0:T(8,128)(2,1)} async-done(((bf16[192,2048]{1,0:T(8,128)(2,1)}), bf16[768,2048]{1,0:T(8,128)(2,1)}) %all-gather.37.cloned.1.call-update) | async-done | bytes 3145744 | tf_op jit(solution)/shard_map/all_gather | solution.py:42
  1116.9 44.3 %while.58 = (s32[]{:T(128)}, f32[768,128]{1,0:T(8,128)}, f32[768,128]{1,0:T(8,128)}, bf16[4,768,128]{1,2,0:T(8,128)(2,1)}, bf16[4,768,128]{2,1,0:T(8,128)(2,1)},...) while((s32[]{:T(128)}, f32[768,128]{1,0:T(8,128)}, ...), condition=%wide.region_29.30_spmd.clone, body=%wide.region_27.29_spmd.clone.sunk | while | flops 763034880 | bytes 28140772 | solution.py:240
  1164.4 5.7 fusion.101
  1170.0 13.7 reduce-scatter.61.cloned.1.call-done
  1183.7 5.5 add_convert_fusion.1
  1189.3 58.6 %reduce-scatter.35.cloned.1.call-done = bf16[192,2048]{1,0:T(8,128)(2,1)} async-done(((bf16[768,2048]{1,0:T(8,128)(2,1)}), bf16[192,2048]{1,0:T(8,128)(2,1)}) %reduce-scatter.35.cloned.1.call-update) | async-done | bytes 786448 | tf_op jit(solution)/shard_map/reduce_scatter | solution.py:56
  1256.2 63.2 %all-gather.39.cloned.1.call-done = bf16[768,2048]{1,0:T(8,128)(2,1)} async-done(((bf16[192,2048]{1,0:T(8,128)(2,1)}), bf16[768,2048]{1,0:T(8,128)(2,1)}) %all-gather.39.cloned.1.call-update) | async-done | bytes 3145744 | tf_op jit(solution)/shard_map/all_gather | solution.py:42
  1319.4 14.7 convert_reduce_fusion.1
  1335.8 10.2 fusion.82
  1346.1 59.0 %reduce-scatter.37.cloned.1.call-done = bf16[192,2048]{1,0:T(8,128)(2,1)} async-done(((bf16[768,2048]{1,0:T(8,128)(2,1)}), bf16[192,2048]{1,0:T(8,128)(2,1)}) %reduce-scatter.37.cloned.1.call-update) | async-done | bytes 786448 | tf_op jit(solution)/shard_map/reduce_scatter | solution.py:56
  1411.3 63.4 %all-gather.41.cloned.1.call-done = bf16[768,2048]{1,0:T(8,128)(2,1)} async-done(((bf16[192,2048]{1,0:T(8,128)(2,1)}), bf16[768,2048]{1,0:T(8,128)(2,1)}) %all-gather.41.cloned.1.call-update) | async-done | bytes 3145744 | tf_op jit(solution)/shard_map/all_gather | solution.py:42
  1480.6 39.8 %while.59 = (s32[]{:T(128)}, f32[768,128]{1,0:T(8,128)}, f32[768,128]{1,0:T(8,128)}, bf16[4,768,128]{1,2,0:T(8,128)(2,1)}, bf16[4,768,128]{2,1,0:T(8,128)(2,1)},...) while((s32[]{:T(128)}, f32[768,128]{1,0:T(8,128)}, ...), condition=%wide.region_39.40_spmd.clone, body=%wide.region_37.39_spmd.clone.sunk | while | flops 763034880 | bytes 28927240 | solution.py:240
  1523.5 13.1 fusion.91
  1545.4 12.6 convolution_convert_fusion
  1558.7 12.6 convolution_convert_fusion.1
  1580.6 10.9 convolution_convert_fusion.2
  1593.4 10.8 convolution_convert_fusion.3
  1610.5 5.4 convolution_convert_fusion.7
  1629.0 12.4 all-to-all-done.2
  1647.6 80.4 %all-reduce.7.cloned.1.call-done = f32[2,8192]{1,0:T(2,128)} async-done(((f32[2,8192]{1,0:T(2,128)}), f32[2,8192]{1,0:T(2,128)}) %all-reduce.7.cloned.1.call-update) | async-done | bytes 65552 | tf_op jit(solution)/shard_map/psum | solution.py:308
  1738.0 27.2 %reduce-scatter.47.cloned.1.call-done = bf16[256,64]{0,1:T(8,128)(2,1)} async-done(((bf16[2048,64]{0,1:T(8,128)(2,1)}), bf16[256,64]{0,1:T(8,128)(2,1)}) %reduce-scatter.47.cloned.1.call-update) | async-done | bytes 32784 | tf_op jit(solution)/shard_map/reduce_scatter | solution.py:277
  1765.2 36.9 %reduce-scatter.45.cloned.1.call-done = bf16[256,64]{0,1:T(8,128)(2,1)} async-done(((bf16[2048,64]{0,1:T(8,128)(2,1)}), bf16[256,64]{0,1:T(8,128)(2,1)}) %reduce-scatter.45.cloned.1.call-update) | async-done | bytes 32784 | tf_op jit(solution)/shard_map/reduce_scatter | solution.py:277
  1803.6 73.3 %reduce-scatter.59.cloned.1.call-done = bf16[2048,256]{1,0:T(8,128)(2,1)} async-done(((bf16[2048,2048]{1,0:T(8,128)(2,1)}), bf16[2048,256]{1,0:T(8,128)(2,1)}) %reduce-scatter.59.cloned.1.call-update) | async-done | bytes 1048592 | tf_op jit(solution)/shard_map/reduce_scatter | solution.py:286
  1876.9 75.0 %reduce-scatter.57.cloned.1.call-done = bf16[2048,256]{1,0:T(8,128)(2,1)} async-done(((bf16[2048,2048]{1,0:T(8,128)(2,1)}), bf16[2048,256]{1,0:T(8,128)(2,1)}) %reduce-scatter.57.cloned.1.call-update) | async-done | bytes 1048592 | tf_op jit(solution)/shard_map/reduce_scatter | solution.py:286
  1955.9 59.2 %reduce-scatter.39.cloned.1.call-done = bf16[192,2048]{1,0:T(8,128)(2,1)} async-done(((bf16[768,2048]{1,0:T(8,128)(2,1)}), bf16[192,2048]{1,0:T(8,128)(2,1)}) %reduce-scatter.39.cloned.1.call-update) | async-done | bytes 786448 | tf_op jit(solution)/shard_map/reduce_scatter | solution.py:56
  2024.5 65.4 %reduce-scatter.55.cloned.1.call-done = bf16[256,2048]{1,0:T(8,128)(2,1)} async-done(((bf16[2048,2048]{1,0:T(8,128)(2,1)}), bf16[256,2048]{1,0:T(8,128)(2,1)}) %reduce-scatter.55.cloned.1.call-update) | async-done | bytes 1048592 | tf_op jit(solution)/shard_map/reduce_scatter | solution.py:283
  2089.9 75.0 %reduce-scatter.53.cloned.1.call-done = bf16[256,2048]{1,0:T(8,128)(2,1)} async-done(((bf16[2048,2048]{1,0:T(8,128)(2,1)}), bf16[256,2048]{1,0:T(8,128)(2,1)}) %reduce-scatter.53.cloned.1.call-update) | async-done | bytes 1048592 | tf_op jit(solution)/shard_map/reduce_scatter | solution.py:283
  2168.8 40.7 %reduce-scatter.51.cloned.1.call-done = bf16[512,256]{1,0:T(8,128)(2,1)} async-done(((bf16[512,2048]{1,0:T(8,128)(2,1)}), bf16[512,256]{1,0:T(8,128)(2,1)}) %reduce-scatter.51.cloned.1.call-update) | async-done | bytes 262160 | tf_op jit(solution)/shard_map/reduce_scatter | solution.py:280
  2209.5 44.9 %reduce-scatter.49.cloned.1.call-done = bf16[512,256]{1,0:T(8,128)(2,1)} async-done(((bf16[512,2048]{1,0:T(8,128)(2,1)}), bf16[512,256]{1,0:T(8,128)(2,1)}) %reduce-scatter.49.cloned.1.call-update) | async-done | bytes 262160 | tf_op jit(solution)/shard_map/reduce_scatter | solution.py:280
  2257.2 41.6 %reduce-scatter.43.cloned.1.call-done = bf16[256,512]{1,0:T(8,128)(2,1)} async-done(((bf16[2048,512]{1,0:T(8,128)(2,1)}), bf16[256,512]{1,0:T(8,128)(2,1)}) %reduce-scatter.43.cloned.1.call-update) | async-done | bytes 262160 | tf_op jit(solution)/shard_map/reduce_scatter | solution.py:274
  2298.8 44.8 %reduce-scatter.41.cloned.1.call-done = bf16[256,512]{1,0:T(8,128)(2,1)} async-done(((bf16[2048,512]{1,0:T(8,128)(2,1)}), bf16[256,512]{1,0:T(8,128)(2,1)}) %reduce-scatter.41.cloned.1.call-update) | async-done | bytes 262160 | tf_op jit(solution)/shard_map/reduce_scatter | solution.py:274
  2345.6 130.5 %all-reduce.9.cloned.1.call-done = (f32[2,2048]{1,0:T(2,128)}, f32[2,2048]{1,0:T(2,128)}, f32[2,2048]{1,0:T(2,128)}, f32[2,256]{1,0:T(2,128)}, f32[2,2048]{1,0:T...) async-done(((f32[2,2048]{1,0:T(2,128)}, f32[2,2048]{1,0:T(2,128)}, f32[2,2048]{1,0:T(2,128)}, f32[2,256]{1,0:T(2,128)}, f32[2,2048]{1,0:T(2,128)}, ...) | async-done | bytes 116752 | tf_op jit(solution)/shard_map/psum | solution.py:308
  (616 shorter events, 339.9 us)
Async XLA Ops:
  9.0 703.2 %copy-start.63 = (s32[192]{0:T(256)}, s32[192]{0:T(256)S(1)}, u32[]{:S(2)}) copy-start(s32[192]{0:T(256)S(1)} %multiply_add_fusion.4) | copy-start | bytes 2308
  9.8 9.8 all-to-all-start
  19.5 16.1 all-to-all-start.1
  23.1 78.2 %all-gather.27.cloned.1.call-start = ((), (), s32[]{:S(2)}) async-start(), calls=%async_computation.25 | async-start | bytes 3932160 | tf_op jit(solution)/shard_map/all_gather | solution.py:38
  36.1 200.0 %copy-start.4 = (f32[192,2048]{1,0:T(8,128)}, f32[192,2048]{1,0:T(8,128)S(1)}, u32[]{:S(2)}) copy-start(f32[192,2048]{1,0:T(8,128)S(1)} %get-tuple-element.604) | copy-start | bytes 4718596
  38.3 92.1 %all-gather.43.cloned.1.call-start = ((), (), s32[]{:S(2)}) async-start(), calls=%async_computation.52 | async-start | bytes 2359296 | tf_op jit(solution)/shard_map/all_gather | solution.py:124
  39.2 130.8 %all-gather.45.cloned.1.call-start = ((), (), s32[]{:S(2)}) async-start(), calls=%async_computation.53 | async-start | bytes 2359296 | tf_op jit(solution)/shard_map/all_gather | solution.py:126
  40.1 196.0 %reduce-scatter.25.cloned.1.call-start = ((), (), s32[]{:S(2)}) async-start(), calls=%async_computation.26 | async-start | bytes 3932160 | tf_op jit(solution)/shard_map/reduce_scatter | solution.py:46
  50.2 69.2 %copy-start.40 = (bf16[1,2048,64]{1,2,0:T(8,128)(2,1)}, bf16[1,2048,64]{1,2,0:T(8,128)(2,1)S(1)}, u32[]{:S(2)}) copy-start(bf16[1,2048,64]{1,2,0:T(8,128)(2,1)S(1)} %all-gather.1) | copy-start | bytes 786436
  175.8 117.1 %all-gather.47.cloned.1.call-start = ((), (), s32[]{:S(2)}) async-start(), calls=%async_computation.54 | async-start | bytes 9437184 | tf_op jit(solution)/shard_map/all_gather | solution.py:127
  179.0 179.4 %all-gather.29.cloned.1.call-start = ((), (), s32[]{:S(2)}) async-start(), calls=%async_computation.27 | async-start | bytes 3932160 | tf_op jit(solution)/shard_map/all_gather | solution.py:38
  237.5 251.5 %copy-start.8 = (f32[192,2048]{1,0:T(8,128)}, f32[192,2048]{1,0:T(8,128)S(1)}, u32[]{:S(2)}) copy-start(f32[192,2048]{1,0:T(8,128)S(1)} %get-tuple-element.560) | copy-start | bytes 4718596
  239.2 176.3 %all-gather.49.cloned.1.call-start = ((), (), s32[]{:S(2)}) async-start(), calls=%async_computation.55 | async-start | bytes 9437184 | tf_op jit(solution)/shard_map/all_gather | solution.py:128
  242.3 246.7 %reduce-scatter.27.cloned.1.call-start = ((), (), s32[]{:S(2)}) async-start(), calls=%async_computation.28 | async-start | bytes 3932160 | tf_op jit(solution)/shard_map/reduce_scatter | solution.py:46
  242.8 172.7 %copy-start.101 = (f32[1,2048]{1,0:T(1,128)}, f32[1,2048]{1,0:T(1,128)S(1)}, u32[]{:S(2)}) copy-start(f32[1,2048]{1,0:T(1,128)S(1)} %get-tuple-element.586) | copy-start | bytes 24580
  242.8 714.0 %copy-start.104 = (f32[1,2048]{1,0:T(1,128)}, f32[1,2048]{1,0:T(1,128)S(1)}, u32[]{:S(2)}) copy-start(f32[1,2048]{1,0:T(1,128)S(1)} %get-tuple-element.585) | copy-start | bytes 24580
  428.6 90.3 %all-gather.51.cloned.1.call-start = ((), (), s32[]{:S(2)}) async-start(), calls=%async_computation.56 | async-start | bytes 2359296 | tf_op jit(solution)/shard_map/all_gather | solution.py:124
  429.3 155.0 %all-gather.31.cloned.1.call-start = ((), (), s32[]{:S(2)}) async-start(), calls=%async_computation.29 | async-start | bytes 3932160 | tf_op jit(solution)/shard_map/all_gather | solution.py:38
  490.5 218.6 %copy-start.2 = (f32[192,2048]{1,0:T(8,128)}, f32[192,2048]{1,0:T(8,128)S(1)}, u32[]{:S(2)}) copy-start(f32[192,2048]{1,0:T(8,128)S(1)} %get-tuple-element.558) | copy-start | bytes 4718596
  490.5 93.9 %copy-start.107 = (f32[1,512]{1,0:T(1,128)S(1)}, f32[1,512]{1,0:T(1,128)}, u32[]{:S(2)}) copy-start(f32[1,512]{1,0:T(1,128)} %get-tuple-element.597) | copy-start | bytes 6148
  490.8 98.8 %copy-start.98 = (f32[192]{0:T(256)}, f32[192]{0:T(256)S(1)}, u32[]{:S(2)}) copy-start(f32[192]{0:T(256)S(1)} %multiply_reduce_fusion.3) | copy-start | bytes 2308
  490.9 98.8 %copy-start.90 = (f32[192]{0:T(256)}, f32[192]{0:T(256)S(1)}, u32[]{:S(2)}) copy-start(f32[192]{0:T(256)S(1)} %fusion.162) | copy-start | bytes 2308
  492.2 152.5 %all-gather.53.cloned.1.call-start = ((), (), s32[]{:S(2)}) async-start(), calls=%async_computation.57 | async-start | bytes 2359296 | tf_op jit(solution)/shard_map/all_gather | solution.py:126
  492.9 216.2 %reduce-scatter.29.cloned.1.call-start = ((), (), s32[]{:S(2)}) async-start(), calls=%async_computation.30 | async-start | bytes 3932160 | tf_op jit(solution)/shard_map/reduce_scatter | solution.py:46
  504.0 87.2 %copy-start.42 = (bf16[1,2048,64]{1,2,0:T(8,128)(2,1)}, bf16[1,2048,64]{1,2,0:T(8,128)(2,1)S(1)}, u32[]{:S(2)}) copy-start(bf16[1,2048,64]{1,2,0:T(8,128)(2,1)S(1)} %all-gather.6) | copy-start | bytes 786436
  650.4 119.8 %all-gather.55.cloned.1.call-start = ((), (), s32[]{:S(2)}) async-start(), calls=%async_computation.58 | async-start | bytes 9437184 | tf_op jit(solution)/shard_map/all_gather | solution.py:127
  651.2 184.6 %all-gather.33.cloned.1.call-start = ((), (), s32[]{:S(2)}) async-start(), calls=%async_computation.31 | async-start | bytes 3932160 | tf_op jit(solution)/shard_map/all_gather | solution.py:38
  710.5 334.4 %copy-start.6 = (f32[192,2048]{1,0:T(8,128)}, f32[192,2048]{1,0:T(8,128)S(1)}, u32[]{:S(2)}) copy-start(f32[192,2048]{1,0:T(8,128)S(1)} %get-tuple-element.556) | copy-start | bytes 4718596
  712.1 187.8 %all-gather.35.cloned.1.call-start = ((), (), s32[]{:S(2)}) async-start(), calls=%async_computation.33 | async-start | bytes 3932160 | tf_op jit(solution)/shard_map/all_gather | solution.py:42
  737.1 308.3 %copy-start.15 = (f32[192,2048]{1,0:T(8,128)}, f32[192,2048]{1,0:T(8,128)S(1)}, u32[]{:S(2)}) copy-start(f32[192,2048]{1,0:T(8,128)S(1)} %get-tuple-element.605) | copy-start | bytes 4718596
  737.2 219.7 %all-gather.57.cloned.1.call-start = ((), (), s32[]{:S(2)}) async-start(), calls=%async_computation.59 | async-start | bytes 9437184 | tf_op jit(solution)/shard_map/all_gather | solution.py:128
  737.7 304.7 %reduce-scatter.33.cloned.1.call-start = ((), (), s32[]{:S(2)}) async-start(), calls=%async_computation.34 | async-start | bytes 3932160 | tf_op jit(solution)/shard_map/reduce_scatter | solution.py:56
  982.0 129.1 %all-gather.37.cloned.1.call-start = ((), (), s32[]{:S(2)}) async-start(), calls=%async_computation.35 | async-start | bytes 3932160 | tf_op jit(solution)/shard_map/all_gather | solution.py:42
  1047.5 136.2 %reduce-scatter.61.cloned.1.call-start = ((), (), s32[]{:S(2)}) async-start(), calls=%async_computation.60 | async-start | bytes 491520
  1164.3 83.6 %reduce-scatter.35.cloned.1.call-start = ((), (), s32[]{:S(2)}) async-start(), calls=%async_computation.36 | async-start | bytes 3932160 | tf_op jit(solution)/shard_map/reduce_scatter | solution.py:56
  1189.2 63.6 %copy-start.16 = (f32[192,2048]{1,0:T(8,128)S(1)}, f32[192,2048]{1,0:T(8,128)}, u32[]{:S(2)}) copy-start(f32[192,2048]{1,0:T(8,128)} %copy-done.15) | copy-start | bytes 4718596
  1189.3 130.1 %all-gather.39.cloned.1.call-start = ((), (), s32[]{:S(2)}) async-start(), calls=%async_computation.37 | async-start | bytes 3932160 | tf_op jit(solution)/shard_map/all_gather | solution.py:42
  1252.9 66.5 %copy-start.102 = (f32[1,2048]{1,0:T(1,128)S(1)}, f32[1,2048]{1,0:T(1,128)}, u32[]{:S(2)}) copy-start(f32[1,2048]{1,0:T(1,128)} %copy-done.101) | copy-start | bytes 24580
  1255.7 149.4 %reduce-scatter.37.cloned.1.call-start = ((), (), s32[]{:S(2)}) async-start(), calls=%async_computation.38 | async-start | bytes 3932160 | tf_op jit(solution)/shard_map/reduce_scatter | solution.py:56
  1346.0 128.7 %all-gather.41.cloned.1.call-start = ((), (), s32[]{:S(2)}) async-start(), calls=%async_computation.39 | async-start | bytes 3932160 | tf_op jit(solution)/shard_map/all_gather | solution.py:42
  1411.1 131.8 %reduce-scatter.63.cloned.1.call-start = ((), (), s32[]{:S(2)}) async-start(), calls=%async_computation.61 | async-start | bytes 491520
  1523.5 97.0 %reduce-scatter.31.cloned.1.call-start = ((), (), s32[]{:S(2)}) async-start(), calls=%async_computation.32 | async-start | bytes 3932160 | tf_op jit(solution)/shard_map/reduce_scatter | solution.py:46
  1536.7 191.2 %all-reduce.7.cloned.1.call-start = ((), (), s32[]{:S(2)}) async-start(), calls=%async_computation.49 | async-start | bytes 131072 | tf_op jit(solution)/shard_map/psum | solution.py:308
  1538.1 227.1 %reduce-scatter.47.cloned.1.call-start = ((), (), s32[]{:S(2)}) async-start(), calls=%async_computation.44 | async-start | bytes 294912 | tf_op jit(solution)/shard_map/reduce_scatter | solution.py:277
  1541.4 260.8 %reduce-scatter.45.cloned.1.call-start = ((), (), s32[]{:S(2)}) async-start(), calls=%async_computation.43 | async-start | bytes 294912 | tf_op jit(solution)/shard_map/reduce_scatter | solution.py:277
  1545.2 331.8 %reduce-scatter.59.cloned.1.call-start = ((), (), s32[]{:S(2)}) async-start(), calls=%async_computation.51 | async-start | bytes 9437184 | tf_op jit(solution)/shard_map/reduce_scatter | solution.py:286
  1558.0 393.9 %reduce-scatter.57.cloned.1.call-start = ((), (), s32[]{:S(2)}) async-start(), calls=%async_computation.50 | async-start | bytes 9437184 | tf_op jit(solution)/shard_map/reduce_scatter | solution.py:286
  1571.3 443.8 %reduce-scatter.39.cloned.1.call-start = ((), (), s32[]{:S(2)}) async-start(), calls=%async_computation.40 | async-start | bytes 3932160 | tf_op jit(solution)/shard_map/reduce_scatter | solution.py:56
  1578.7 511.2 %reduce-scatter.55.cloned.1.call-start = ((), (), s32[]{:S(2)}) async-start(), calls=%async_computation.48 | async-start | bytes 9437184 | tf_op jit(solution)/shard_map/reduce_scatter | solution.py:283
  1591.5 573.4 %reduce-scatter.53.cloned.1.call-start = ((), (), s32[]{:S(2)}) async-start(), calls=%async_computation.47 | async-start | bytes 9437184 | tf_op jit(solution)/shard_map/reduce_scatter | solution.py:283
  1604.2 605.2 %reduce-scatter.51.cloned.1.call-start = ((), (), s32[]{:S(2)}) async-start(), calls=%async_computation.46 | async-start | bytes 2359296 | tf_op jit(solution)/shard_map/reduce_scatter | solution.py:280
  1610.4 643.9 %reduce-scatter.49.cloned.1.call-start = ((), (), s32[]{:S(2)}) async-start(), calls=%async_computation.45 | async-start | bytes 2359296 | tf_op jit(solution)/shard_map/reduce_scatter | solution.py:280
  1616.0 682.8 %reduce-scatter.43.cloned.1.call-start = ((), (), s32[]{:S(2)}) async-start(), calls=%async_computation.42 | async-start | bytes 2359296 | tf_op jit(solution)/shard_map/reduce_scatter | solution.py:274
  1624.3 106.3 %copy-start.11 = (bf16[768,2048]{1,0:T(8,128)(2,1)S(1)}, bf16[768,2048]{1,0:T(8,128)(2,1)}, u32[]{:S(2)}) copy-start(bf16[768,2048]{1,0:T(8,128)(2,1)} %all-gather.27.cloned.1.call-done) | copy-start | bytes 9437188
  1624.3 17.1 all-to-all-start.2
  1628.8 714.8 %reduce-scatter.41.cloned.1.call-start = ((), (), s32[]{:S(2)}) async-start(), calls=%async_computation.41 | async-start | bytes 2359296 | tf_op jit(solution)/shard_map/reduce_scatter | solution.py:274
  1952.0 63.2 %copy-start.5 = (f32[192,2048]{1,0:T(8,128)S(1)}, f32[192,2048]{1,0:T(8,128)}, u32[]{:S(2)}) copy-start(f32[192,2048]{1,0:T(8,128)} %copy-done.4) | copy-start | bytes 4718596
  1952.0 63.2 %copy-start.55 = (f32[1,2048]{1,0:T(1,128)S(1)}, f32[1,2048]{1,0:T(1,128)}, u32[]{:S(2)}) copy-start(f32[1,2048]{1,0:T(1,128)} %copy-done.54) | copy-start | bytes 24580
  1952.0 63.2 %copy-start.62 = (f32[192]{0:T(256)S(1)}, f32[192]{0:T(256)}, u32[]{:S(2)}) copy-start(f32[192]{0:T(256)} %copy-done.61) | copy-start | bytes 2308
  2020.8 457.8 %all-to-all-start.4 = ((bf16[8,24,2048]{2,1,0:T(8,128)(2,1)}), bf16[8,24,2048]{2,1,0:T(8,128)(2,1)S(1)}, u32[]{:S(2)}, u32[]{:S(2)}) async-start(bf16[8,24,2048]{2,1,0:T(8,128)(2,1)} %bitcast.336), calls=%async_computation.12 | async-start | bytes 1572864 | tf_op jit(solution)/shard_map/all_to_all | solution.py:331
  2024.5 451.7 %all-reduce.9.cloned.1.call-start = ((), (), s32[]{:S(2)}) async-start(), calls=%async_computation.62 | async-start | bytes 233472 | tf_op jit(solution)/shard_map/psum | solution.py:308
  2164.9 91.6 %copy-start.69 = (f32[2048]{0:T(1024)S(1)}, f32[2048]{0:T(1024)}, u32[]{:S(2)}) copy-start(f32[2048]{0:T(1024)} %get-tuple-element.464) | copy-start | bytes 24580
  2164.9 91.6 %copy-start.70 = (f32[2048]{0:T(1024)S(1)}, f32[2048]{0:T(1024)}, u32[]{:S(2)}) copy-start(f32[2048]{0:T(1024)} %get-tuple-element.454) | copy-start | bytes 24580
  2254.4 233.5 %copy-start.1 = (bf16[192,2048]{1,0:T(8,128)(2,1)S(1)}, bf16[192,2048]{1,0:T(8,128)(2,1)}, u32[]{:S(2)}) copy-start(bf16[192,2048]{1,0:T(8,128)(2,1)} %param.26) | copy-start | bytes 2359300
  (114 other events, 1216.0 us)
Sparse Core Ops, SparseCore 0:
  38.4 62.8 all-gather.26
  103.8 26.5 all-gather.42
  132.8 28.1 all-gather.44
  175.9 60.1 reduce-scatter.24
  238.4 54.4 all-gather.46
  294.9 63.4 all-gather.28
  360.9 54.5 all-gather.48
  428.7 60.2 reduce-scatter.26
  490.9 27.9 all-gather.50
  520.9 63.4 all-gather.30
  586.3 26.8 all-gather.52
  650.5 58.4 reduce-scatter.28
  710.9 59.2 all-gather.54
  772.2 63.4 all-gather.32
  837.7 62.1 all-gather.34
  902.2 54.5 all-gather.56
  982.1 60.2 reduce-scatter.32
  1047.6 63.5 all-gather.36
  1164.4 19.2 reduce-scatter.60
  1189.4 58.5 reduce-scatter.34
  1255.8 63.5 all-gather.38
  1346.2 58.8 reduce-scatter.36
  1411.2 63.5 all-gather.40
  1523.6 19.2 reduce-scatter.62
  1545.7 58.5 reduce-scatter.30
  1610.3 117.5 all-reduce.6
  1730.8 34.3 reduce-scatter.46
  1768.5 33.5 reduce-scatter.44
  1805.6 71.2 reduce-scatter.58
  1880.6 71.2 reduce-scatter.56
  1954.8 60.2 reduce-scatter.38
  2018.6 71.2 reduce-scatter.54
  2093.6 71.2 reduce-scatter.52
  2168.2 41.2 reduce-scatter.50
  2213.1 41.2 reduce-scatter.48
  2257.5 41.2 reduce-scatter.42
  2302.2 41.2 reduce-scatter.40
  2351.1 124.9 all-reduce.8
where the time goes:
time: 2510 us; the launch traced here: 2490 us
  waiting for transfers between devices  1890 us (75%)
  matrix products  350 us (14%)
  other arithmetic  79.2 us (3%)
  blocking collectives  72.6 us (3%)
  local copies, waits for them, and re-layouts  65.7 us (3%)
    all_gather x4, waiting for transfers between devices, rows_gather(): return lax.all_gather(values, 'tensor', axis=0, tiled=True)  247 us
    all_gather x4, waiting for transfers between devices, grad_gather(): return lax.all_gather(values, 'tensor', axis=0, tiled=True)  242 us
    reduce_scatter x4, waiting for transfers between devices, grad_scatter(): lax.psum_scatter(running.astype(jnp.bfloat16), 'tensor', scatter_dimensio...  237 us
    psum x2, waiting for transfers between devices, local(): lax.psum((smalls[0], smalls[1], smalls[2], smalls[3], smalls[4], smalls[5...  211 us
    reduce_scatter x4, waiting for transfers between devices, rows_scatter(): lax.psum_scatter(matmul(left, right).astype(jnp.bfloat16), 'tensor', scat...  174 us
    reduce_scatter x2, waiting for transfers between devices, local(): lax.psum_scatter(down_grad.astype(jnp.bfloat16), 'dp', scatter_dimension=...  148 us
    reduce_scatter x2, waiting for transfers between devices, local(): lax.psum_scatter(up_grad.astype(jnp.bfloat16), 'dp', scatter_dimension=0,...  140 us
    dot_general x34, matrix products, contract_cols(): lax.dot_general(left, right, (((1,), (1,)), ((), ())), preferred_element_...  118 us
  transfers between devices with their start and end apart: 42, of which 38 were waited for; matrix products, arithmetic and copies ran while one was open for 11% of the time, Pallas kernels for 0%

commit v1 on v0

--- a/solution.py
+++ b/solution.py
@@ -1,3 +1,4 @@
+import functools
 import jax
 import jax.numpy as jnp
 from jax import lax
@@ -5,6 +6,30 @@
 
 HEAD = 128
 EPSILON = 1e-05
+
+
+def rest_map_now(xs, dev_axis):
+    gallery = []
+    nodes = lax.psum(1, axis_name=dev_axis)
+    for q in range(nodes):
+        gallery.append((q, (q + 1) % nodes))
+    row_list = []
+    for q in range(nodes):
+        row_list.append((q, (q - 1) % nodes))
+    y1, block_next = ([xs], [xs])
+    for _ in range(nodes // 2):
+        step_out = lax.ppermute(y1[-1], perm=gallery, axis_name=dev_axis)
+        y1.append(step_out)
+    for _ in range((nodes - 1) // 2):
+        r2 = lax.ppermute(block_next[-1], axis_name=dev_axis, perm=row_list)
+        block_next.append(r2)
+    built = jnp.concatenate([*y1[::-1], *block_next[1:]], axis=0)
+    b_now = lax.axis_index(dev_axis)
+    o_now = jnp.roll(built, shift=(b_now - nodes // 2) * xs.shape[0], axis=0)
+    return o_now
+
+
+recast_rates = functools.partial(rest_map_now, dev_axis="tensor")
 
 
 def layer_norm(values, scales, offsets):
@@ -35,7 +60,7 @@
 
 
 def rows_gather(values):
-    return lax.all_gather(values, "tensor", axis=0, tiled=True)
+    return recast_rates(values)
 
 
 def grad_gather(values):

time: 2510 us -> 2340 us (0.932)
  waiting for transfers between devices: 1890 us -> 1610 us
  starting transfers between devices: 20.6 us -> 87.9 us
  other arithmetic: 79.2 us -> 137 us
    all_gather x4 -> x0, waiting for transfers between devices: 247 us -> none  [rows_gather(): return lax.all_gather(values, 'tensor', axis=0, tiled=True)]
    ppermute x0 -> x12, waiting for transfers between devices: none -> 123 us  [the longest x8 120 us: rest_map_now(): step_out = lax.ppermute(y1[-1], perm=gallery, axis_name=dev_axis)]
    all_gather x2, waiting for transfers between devices: 82.3 us -> 0.02 us  [local(): lax.all_gather(up_weight[layer_index], 'dp', axis=0, tiled=True)]
    ppermute x0 -> x12, starting transfers between devices: none -> 70.5 us  [the longest x8 59.7 us: rest_map_now(): step_out = lax.ppermute(y1[-1], perm=gallery, axis_name=dev_axis)]
    concatenate x0 -> x4, other arithmetic: none -> 61.2 us  [rest_map_now(): o_now = jnp.roll(built, shift=(b_now - nodes // 2) * xs.shape[0], axis=0)]
    all_gather x2, waiting for transfers between devices: 25.5 us -> 0.04 us  [local(): lax.all_gather(query_weight[layer_index], 'dp', axis=0, tiled=True)]
  transfers between devices with their start and end apart: 42 -> 50, of which waited for: 38 -> 40; matrix products, arithmetic and copies ran while one was open for 11% -> 14% of each run, Pallas kernels for 0% -> 0%
where the time goes in v1:
time: 2340 us
  waiting for transfers between devices  1610 us (69%)
  matrix products  356 us (15%)
  other arithmetic  137 us (6%)
  starting transfers between devices  87.9 us (4%)
  local copies, waits for them, and re-layouts  67.2 us (3%)
  blocking collectives  64 us (3%)
    reduce_scatter x4, waiting for transfers between devices, grad_scatter(): lax.psum_scatter(running.astype(jnp.bfloat16), 'tensor', scatter_dimensio...  236 us
    all_gather x4, waiting for transfers between devices, grad_gather(): return lax.all_gather(values, 'tensor', axis=0, tiled=True)  228 us
    psum x2, waiting for transfers between devices, local(): lax.psum((smalls[0], smalls[1], smalls[2], smalls[3], smalls[4], smalls[5...  208 us
    reduce_scatter x4, waiting for transfers between devices, rows_scatter(): lax.psum_scatter(matmul(left, right).astype(jnp.bfloat16), 'tensor', scat...  153 us
    reduce_scatter x2, waiting for transfers between devices, local(): lax.psum_scatter(down_grad.astype(jnp.bfloat16), 'dp', scatter_dimension=...  148 us
    reduce_scatter x2, waiting for transfers between devices, local(): lax.psum_scatter(up_grad.astype(jnp.bfloat16), 'dp', scatter_dimension=0,...  141 us
    dot_general x30, matrix products, contract_rows(): lax.dot_general(left, right, (((0,), (0,)), ((), ())), preferred_element_...  121 us
    ppermute x8, waiting for transfers between devices, rest_map_now(): step_out = lax.ppermute(y1[-1], perm=gallery, axis_name=dev_axis)  120 us
  transfers between devices with their start and end apart: 50, of which 40 were waited for; matrix products, arithmetic and copies ran while one was open for 14% of the time, Pallas kernels for 0%

profile of v1, /device:TPU:0, one launch (start us, length us, event | category | flops | bytes accessed | tf_op | source)
XLA Modules:
  0.0 2337.2 jit_solution(8438404686743758265)
XLA Ops:
  27.6 13.0 all-to-all-done.1
  47.1 17.4 collective-permute-done
  64.5 12.7 collective-permute-start.1
  77.8 9.1 all-gather.1
  93.5 15.8 fusion.122
  112.3 14.8 all_gather.60
  132.9 33.6 %while.56 = (s32[]{:T(128)}, bf16[4,768,128]{1,2,0:T(8,128)(2,1)S(1)}, f32[4,768]{1,0:T(4,128)}, bf16[4,768,128]{2,1,0:T(8,128)(2,1)S(1)}, bf16[768,128]{1,0:T(8...) while((s32[]{:T(128)}, ...), condition=%wide.region_9.11_spmd.clone, body=%wide.region_6.10_spmd.clone.sunk | while | flops 308477184 | bytes 8108645 | solution.py:177
  178.8 54.7 %reduce-scatter.25.cloned.1.call-done = bf16[192,2048]{1,0:T(8,128)(2,1)} async-done(((bf16[768,2048]{1,0:T(8,128)(2,1)}), bf16[192,2048]{1,0:T(8,128)(2,1)}) %reduce-scatter.25.cloned.1.call-update) | async-done | bytes 786448 | tf_op jit(solution)/shard_map/reduce_scatter | solution.py:71
  239.6 18.5 collective-permute-done.3
  258.1 14.2 collective-permute-start.4
  273.7 16.8 collective-permute-done.4
  290.4 15.8 fusion.115
  306.3 11.7 fusion.66
  317.9 30.1 %all-gather.37.cloned.1.call-done = bf16[1,2048,2048]{2,1,0:T(8,128)(2,1)} async-done(((bf16[1,2048,256]{2,1,0:T(8,128)(2,1)}), bf16[1,2048,2048]{2,1,0:T(8,128)(2,1)}) %all-gather.37.cloned.1.call-update) | async-done | bytes 8388624 | tf_op jit(solution)/shard_map/all_gather | solution.py:153
  348.0 13.6 fusion.85
  363.1 59.0 %reduce-scatter.27.cloned.1.call-done = bf16[192,2048]{1,0:T(8,128)(2,1)} async-done(((bf16[768,2048]{1,0:T(8,128)(2,1)}), bf16[192,2048]{1,0:T(8,128)(2,1)}) %reduce-scatter.27.cloned.1.call-update) | async-done | bytes 786448 | tf_op jit(solution)/shard_map/reduce_scatter | solution.py:71
  428.1 18.6 collective-permute-done.6
  446.7 13.9 collective-permute-start.7
  460.7 9.9 all-gather.6
  470.7 8.4 collective-permute-done.7
  479.1 13.8 fusion.108
  502.7 14.2 all_gather.66
  518.6 33.9 %while.57 = (s32[]{:T(128)}, bf16[4,768,128]{1,2,0:T(8,128)(2,1)S(1)}, f32[4,768]{1,0:T(4,128)}, bf16[4,768,128]{2,1,0:T(8,128)(2,1)S(1)}, bf16[768,128]{1,0:T(8...) while((s32[]{:T(128)}, ...), condition=%wide.region_19.21_spmd.clone, body=%wide.region_16.20_spmd.clone.sunk | while | flops 308477184 | bytes 8108645 | solution.py:177
  559.8 16.0 all_to_all.57
  578.7 39.4 %reduce-scatter.29.cloned.1.call-done = bf16[192,2048]{1,0:T(8,128)(2,1)} async-done(((bf16[768,2048]{1,0:T(8,128)(2,1)}), bf16[192,2048]{1,0:T(8,128)(2,1)}) %reduce-scatter.29.cloned.1.call-update) | async-done | bytes 786448 | tf_op jit(solution)/shard_map/reduce_scatter | solution.py:71
  624.1 18.5 collective-permute-done.9
  642.6 14.0 collective-permute-start.10
  658.2 16.8 collective-permute-done.10
  675.0 15.8 fusion.101
  690.8 11.7 fusion.58
  702.5 37.5 %all-gather.23.cloned.1.call-done = bf16[768,2048]{1,0:T(8,128)(2,1)} async-done(((bf16[192,2048]{1,0:T(8,128)(2,1)}), bf16[768,2048]{1,0:T(8,128)(2,1)}) %all-gather.23.cloned.1.call-update) | async-done | bytes 3145744 | tf_op jit(solution)/shard_map/all_gather | solution.py:67
  740.0 56.9 %all-gather.45.cloned.1.call-done = bf16[1,2048,2048]{2,1,0:T(8,128)(2,1)} async-done(((bf16[1,2048,256]{2,1,0:T(8,128)(2,1)}), bf16[1,2048,2048]{2,1,0:T(8,128)(2,1)}) %all-gather.45.cloned.1.call-update) | async-done | bytes 8388624 | tf_op jit(solution)/shard_map/all_gather | solution.py:153
  796.9 15.6 convert_reduce_fusion
  814.2 8.1 fusion.88
  822.4 60.3 %reduce-scatter.33.cloned.1.call-done = bf16[192,2048]{1,0:T(8,128)(2,1)} async-done(((bf16[768,2048]{1,0:T(8,128)(2,1)}), bf16[192,2048]{1,0:T(8,128)(2,1)}) %reduce-scatter.33.cloned.1.call-update) | async-done | bytes 786448 | tf_op jit(solution)/shard_map/reduce_scatter | solution.py:81
  888.9 63.6 %all-gather.25.cloned.1.call-done = bf16[768,2048]{1,0:T(8,128)(2,1)} async-done(((bf16[192,2048]{1,0:T(8,128)(2,1)}), bf16[768,2048]{1,0:T(8,128)(2,1)}) %all-gather.25.cloned.1.call-update) | async-done | bytes 3145744 | tf_op jit(solution)/shard_map/all_gather | solution.py:67
  958.2 44.8 %while.58 = (s32[]{:T(128)}, f32[768,128]{1,0:T(8,128)}, f32[768,128]{1,0:T(8,128)}, bf16[4,768,128]{1,2,0:T(8,128)(2,1)}, bf16[4,768,128]{2,1,0:T(8,128)(2,1)},...) while((s32[]{:T(128)}, f32[768,128]{1,0:T(8,128)}, ...), condition=%wide.region_29.31_spmd.clone, body=%wide.region_27.30_spmd.clone.sunk | while | flops 763034880 | bytes 28140772 | solution.py:265
  1011.9 13.7 reduce-scatter.61.cloned.1.call-done
  1031.2 58.5 %reduce-scatter.35.cloned.1.call-done = bf16[192,2048]{1,0:T(8,128)(2,1)} async-done(((bf16[768,2048]{1,0:T(8,128)(2,1)}), bf16[192,2048]{1,0:T(8,128)(2,1)}) %reduce-scatter.35.cloned.1.call-update) | async-done | bytes 786448 | tf_op jit(solution)/shard_map/reduce_scatter | solution.py:81
  1097.6 63.6 %all-gather.27.cloned.1.call-done = bf16[768,2048]{1,0:T(8,128)(2,1)} async-done(((bf16[192,2048]{1,0:T(8,128)(2,1)}), bf16[768,2048]{1,0:T(8,128)(2,1)}) %all-gather.27.cloned.1.call-update) | async-done | bytes 3145744 | tf_op jit(solution)/shard_map/all_gather | solution.py:67
  1161.2 15.4 convert_reduce_fusion.1
  1178.2 10.3 fusion.82
  1188.6 59.0 %reduce-scatter.37.cloned.1.call-done = bf16[192,2048]{1,0:T(8,128)(2,1)} async-done(((bf16[768,2048]{1,0:T(8,128)(2,1)}), bf16[192,2048]{1,0:T(8,128)(2,1)}) %reduce-scatter.37.cloned.1.call-update) | async-done | bytes 786448 | tf_op jit(solution)/shard_map/reduce_scatter | solution.py:81
  1254.2 63.6 %all-gather.29.cloned.1.call-done = bf16[768,2048]{1,0:T(8,128)(2,1)} async-done(((bf16[192,2048]{1,0:T(8,128)(2,1)}), bf16[768,2048]{1,0:T(8,128)(2,1)}) %all-gather.29.cloned.1.call-update) | async-done | bytes 3145744 | tf_op jit(solution)/shard_map/all_gather | solution.py:67
  1323.5 40.1 %while.59 = (s32[]{:T(128)}, f32[768,128]{1,0:T(8,128)}, f32[768,128]{1,0:T(8,128)}, bf16[4,768,128]{1,2,0:T(8,128)(2,1)}, bf16[4,768,128]{2,1,0:T(8,128)(2,1)},...) while((s32[]{:T(128)}, f32[768,128]{1,0:T(8,128)}, ...), condition=%wide.region_39.41_spmd.clone, body=%wide.region_37.40_spmd.clone.sunk | while | flops 763034880 | bytes 28927240 | solution.py:265
  1366.7 13.1 fusion.91
  1389.5 14.5 convolution_convert_fusion
  1406.0 14.9 convolution_convert_fusion.1
  1430.1 10.9 convolution_convert_fusion.2
  1442.9 11.1 convolution_convert_fusion.3
  1477.0 12.7 all-to-all-done.2
  1493.7 77.0 %all-reduce.7.cloned.1.call-done = f32[2,8192]{1,0:T(2,128)} async-done(((f32[2,8192]{1,0:T(2,128)}), f32[2,8192]{1,0:T(2,128)}) %all-reduce.7.cloned.1.call-update) | async-done | bytes 65552 | tf_op jit(solution)/shard_map/psum | solution.py:333
  1581.0 27.1 %reduce-scatter.47.cloned.1.call-done = bf16[256,64]{0,1:T(8,128)(2,1)} async-done(((bf16[2048,64]{0,1:T(8,128)(2,1)}), bf16[256,64]{0,1:T(8,128)(2,1)}) %reduce-scatter.47.cloned.1.call-update) | async-done | bytes 32784 | tf_op jit(solution)/shard_map/reduce_scatter | solution.py:302
  1608.1 36.8 %reduce-scatter.45.cloned.1.call-done = bf16[256,64]{0,1:T(8,128)(2,1)} async-done(((bf16[2048,64]{0,1:T(8,128)(2,1)}), bf16[256,64]{0,1:T(8,128)(2,1)}) %reduce-scatter.45.cloned.1.call-update) | async-done | bytes 32784 | tf_op jit(solution)/shard_map/reduce_scatter | solution.py:302
  1646.4 73.4 %reduce-scatter.59.cloned.1.call-done = bf16[2048,256]{1,0:T(8,128)(2,1)} async-done(((bf16[2048,2048]{1,0:T(8,128)(2,1)}), bf16[2048,256]{1,0:T(8,128)(2,1)}) %reduce-scatter.59.cloned.1.call-update) | async-done | bytes 1048592 | tf_op jit(solution)/shard_map/reduce_scatter | solution.py:311
  1719.8 75.0 %reduce-scatter.57.cloned.1.call-done = bf16[2048,256]{1,0:T(8,128)(2,1)} async-done(((bf16[2048,2048]{1,0:T(8,128)(2,1)}), bf16[2048,256]{1,0:T(8,128)(2,1)}) %reduce-scatter.57.cloned.1.call-update) | async-done | bytes 1048592 | tf_op jit(solution)/shard_map/reduce_scatter | solution.py:311
  1798.7 58.5 %reduce-scatter.39.cloned.1.call-done = bf16[192,2048]{1,0:T(8,128)(2,1)} async-done(((bf16[768,2048]{1,0:T(8,128)(2,1)}), bf16[192,2048]{1,0:T(8,128)(2,1)}) %reduce-scatter.39.cloned.1.call-update) | async-done | bytes 786448 | tf_op jit(solution)/shard_map/reduce_scatter | solution.py:81
  1866.6 65.4 %reduce-scatter.55.cloned.1.call-done = bf16[256,2048]{1,0:T(8,128)(2,1)} async-done(((bf16[2048,2048]{1,0:T(8,128)(2,1)}), bf16[256,2048]{1,0:T(8,128)(2,1)}) %reduce-scatter.55.cloned.1.call-update) | async-done | bytes 1048592 | tf_op jit(solution)/shard_map/reduce_scatter | solution.py:308
  1932.0 75.2 %reduce-scatter.53.cloned.1.call-done = bf16[256,2048]{1,0:T(8,128)(2,1)} async-done(((bf16[2048,2048]{1,0:T(8,128)(2,1)}), bf16[256,2048]{1,0:T(8,128)(2,1)}) %reduce-scatter.53.cloned.1.call-update) | async-done | bytes 1048592 | tf_op jit(solution)/shard_map/reduce_scatter | solution.py:308
  2011.1 40.5 %reduce-scatter.51.cloned.1.call-done = bf16[512,256]{1,0:T(8,128)(2,1)} async-done(((bf16[512,2048]{1,0:T(8,128)(2,1)}), bf16[512,256]{1,0:T(8,128)(2,1)}) %reduce-scatter.51.cloned.1.call-update) | async-done | bytes 262160 | tf_op jit(solution)/shard_map/reduce_scatter | solution.py:305
  2051.6 44.9 %reduce-scatter.49.cloned.1.call-done = bf16[512,256]{1,0:T(8,128)(2,1)} async-done(((bf16[512,2048]{1,0:T(8,128)(2,1)}), bf16[512,256]{1,0:T(8,128)(2,1)}) %reduce-scatter.49.cloned.1.call-update) | async-done | bytes 262160 | tf_op jit(solution)/shard_map/reduce_scatter | solution.py:305
  2099.2 41.8 %reduce-scatter.43.cloned.1.call-done = bf16[256,512]{1,0:T(8,128)(2,1)} async-done(((bf16[2048,512]{1,0:T(8,128)(2,1)}), bf16[256,512]{1,0:T(8,128)(2,1)}) %reduce-scatter.43.cloned.1.call-update) | async-done | bytes 262160 | tf_op jit(solution)/shard_map/reduce_scatter | solution.py:299
  2141.0 44.8 %reduce-scatter.41.cloned.1.call-done = bf16[256,512]{1,0:T(8,128)(2,1)} async-done(((bf16[2048,512]{1,0:T(8,128)(2,1)}), bf16[256,512]{1,0:T(8,128)(2,1)}) %reduce-scatter.41.cloned.1.call-update) | async-done | bytes 262160 | tf_op jit(solution)/shard_map/reduce_scatter | solution.py:299
  2187.8 130.6 %all-reduce.9.cloned.1.call-done = (f32[2,2048]{1,0:T(2,128)}, f32[2,2048]{1,0:T(2,128)}, f32[2,2048]{1,0:T(2,128)}, f32[2,256]{1,0:T(2,128)}, f32[2,2048]{1,0:T...) async-done(((f32[2,2048]{1,0:T(2,128)}, f32[2,2048]{1,0:T(2,128)}, f32[2,2048]{1,0:T(2,128)}, f32[2,256]{1,0:T(2,128)}, f32[2,2048]{1,0:T(2,128)}, ...) | async-done | bytes 116752 | tf_op jit(solution)/shard_map/psum | solution.py:333
  (632 shorter events, 397.3 us)
Async XLA Ops:
  7.2 120.2 %all-gather.31.cloned.1.call-start = ((), (), s32[]{:S(2)}) async-start(), calls=%async_computation.48 | async-start | bytes 2359296 | tf_op jit(solution)/shard_map/all_gather | solution.py:149
  10.9 548.0 %copy-start.61 = (s32[192]{0:T(256)}, s32[192]{0:T(256)S(1)}, u32[]{:S(2)}) copy-start(s32[192]{0:T(256)S(1)} %multiply_add_fusion.4) | copy-start | bytes 2308
  11.7 9.8 all-to-all-start
  21.5 19.1 all-to-all-start.1
  25.0 141.6 %all-gather.33.cloned.1.call-start = ((), (), s32[]{:S(2)}) async-start(), calls=%async_computation.49 | async-start | bytes 2359296 | tf_op jit(solution)/shard_map/all_gather | solution.py:151
  41.0 192.5 %copy-start.4 = (f32[192,2048]{1,0:T(8,128)}, f32[192,2048]{1,0:T(8,128)S(1)}, u32[]{:S(2)}) copy-start(f32[192,2048]{1,0:T(8,128)S(1)} %get-tuple-element.605) | copy-start | bytes 4718596
  42.1 22.4 collective-permute-start
  44.7 188.8 %reduce-scatter.25.cloned.1.call-start = ((), (), s32[]{:S(2)}) async-start(), calls=%async_computation.25 | async-start | bytes 3932160 | tf_op jit(solution)/shard_map/reduce_scatter | solution.py:71
  44.8 43.4 %collective-permute-start.2 = (bf16[192,2048]{1,0:T(8,128)(2,1)S(1)}, bf16[192,2048]{1,0:T(8,128)(2,1)S(1)}, u32[]{:S(2)}, u32[]{:S(2)}) collective-permute-start(bf16[192,2048]{1,0:T(8,128)(2,1)S(1)} %add_convert_fusion.9), channel_id=1, source_target_pairs={{0,3},{1,0},{2,1},{3,2},{4,7},{5,4},{6,5},{7,6},{8,11},{9,8},{10,9... | collective-permute-start | bytes 2359304 | tf_op jit(solution)/shard_map/ppermute | solution.py:24
  64.5 29.0 %collective-permute-start.1 = (bf16[192,2048]{1,0:T(8,128)(2,1)S(1)}, bf16[192,2048]{1,0:T(8,128)(2,1)S(1)}, u32[]{:S(2)}, u32[]{:S(2)}) collective-permute-start(bf16[192,2048]{1,0:T(8,128)(2,1)S(1)} %collective-permute-done), channel_id=1, source_target_pairs={{0,1},{1,2},{2,3},{3,0},{4,5},{5,6},{6,7},{7,4},{8,9},{9,10},{10,1... | collective-permute-start | bytes 2359304 | tf_op jit(solution)/shard_map/ppermute | solution.py:21
  172.4 133.9 %all-gather.35.cloned.1.call-start = ((), (), s32[]{:S(2)}) async-start(), calls=%async_computation.50 | async-start | bytes 9437184 | tf_op jit(solution)/shard_map/all_gather | solution.py:152
  175.6 172.4 %all-gather.37.cloned.1.call-start = ((), (), s32[]{:S(2)}) async-start(), calls=%async_computation.51 | async-start | bytes 9437184 | tf_op jit(solution)/shard_map/all_gather | solution.py:153
  178.6 243.4 %reduce-scatter.27.cloned.1.call-start = ((), (), s32[]{:S(2)}) async-start(), calls=%async_computation.26 | async-start | bytes 3932160 | tf_op jit(solution)/shard_map/reduce_scatter | solution.py:71
  235.0 187.1 %copy-start.8 = (f32[192,2048]{1,0:T(8,128)}, f32[192,2048]{1,0:T(8,128)S(1)}, u32[]{:S(2)}) copy-start(f32[192,2048]{1,0:T(8,128)S(1)} %get-tuple-element.561) | copy-start | bytes 4718596
  235.0 71.2 %copy-start.73 = (f32[192]{0:T(256)}, f32[192]{0:T(256)S(1)}, u32[]{:S(2)}) copy-start(f32[192]{0:T(256)S(1)} %broadcast_multiply_fusion.2) | copy-start | bytes 2308
  235.7 22.3 collective-permute-start.3
  236.8 36.9 %collective-permute-start.5 = (bf16[192,2048]{1,0:T(8,128)(2,1)S(1)}, bf16[192,2048]{1,0:T(8,128)(2,1)S(1)}, u32[]{:S(2)}, u32[]{:S(2)}) collective-permute-start(bf16[192,2048]{1,0:T(8,128)(2,1)S(1)} %add_convert_fusion.7), channel_id=1, source_target_pairs={{0,3},{1,0},{2,1},{3,2},{4,7},{5,4},{6,5},{7,6},{8,11},{9,8},{10,9... | collective-permute-start | bytes 2359304 | tf_op jit(solution)/shard_map/ppermute | solution.py:24
  258.1 32.4 %collective-permute-start.4 = (bf16[192,2048]{1,0:T(8,128)(2,1)S(1)}, bf16[192,2048]{1,0:T(8,128)(2,1)S(1)}, u32[]{:S(2)}, u32[]{:S(2)}) collective-permute-start(bf16[192,2048]{1,0:T(8,128)(2,1)S(1)} %collective-permute-done.3), channel_id=1, source_target_pairs={{0,1},{1,2},{2,3},{3,0},{4,5},{5,6},{6,7},{7,4},{8,9},{9,10},{10,1... | collective-permute-start | bytes 2359304 | tf_op jit(solution)/shard_map/ppermute | solution.py:21
  272.3 75.7 %copy-start.101 = (f32[1,2048]{1,0:T(1,128)}, f32[1,2048]{1,0:T(1,128)S(1)}, u32[]{:S(2)}) copy-start(f32[1,2048]{1,0:T(1,128)S(1)} %get-tuple-element.587) | copy-start | bytes 24580
  272.3 524.6 %copy-start.104 = (f32[1,2048]{1,0:T(1,128)}, f32[1,2048]{1,0:T(1,128)S(1)}, u32[]{:S(2)}) copy-start(f32[1,2048]{1,0:T(1,128)S(1)} %get-tuple-element.586) | copy-start | bytes 24580
  361.7 131.2 %all-gather.39.cloned.1.call-start = ((), (), s32[]{:S(2)}) async-start(), calls=%async_computation.52 | async-start | bytes 2359296 | tf_op jit(solution)/shard_map/all_gather | solution.py:149
  362.4 190.1 %all-gather.41.cloned.1.call-start = ((), (), s32[]{:S(2)}) async-start(), calls=%async_computation.53 | async-start | bytes 2359296 | tf_op jit(solution)/shard_map/all_gather | solution.py:151
  423.5 194.6 %copy-start.2 = (f32[192,2048]{1,0:T(8,128)}, f32[192,2048]{1,0:T(8,128)S(1)}, u32[]{:S(2)}) copy-start(f32[192,2048]{1,0:T(8,128)S(1)} %get-tuple-element.559) | copy-start | bytes 4718596
  424.3 22.5 collective-permute-start.6
  425.3 45.3 %collective-permute-start.8 = (bf16[192,2048]{1,0:T(8,128)(2,1)S(1)}, bf16[192,2048]{1,0:T(8,128)(2,1)}, u32[]{:S(2)}, u32[]{:S(2)}) collective-permute-start(bf16[192,2048]{1,0:T(8,128)(2,1)S(1)} %add_convert_fusion.6), channel_id=1, source_target_pairs={{0,3},{1,0},{2,1},{3,2},{4,7},{5,4},{6,5},{7,6},{8,11},{9,8},{10,9... | collective-permute-start | bytes 2359304 | tf_op jit(solution)/shard_map/ppermute | solution.py:24
  446.7 32.4 %collective-permute-start.7 = (bf16[192,2048]{1,0:T(8,128)(2,1)}, bf16[192,2048]{1,0:T(8,128)(2,1)}, u32[]{:S(2)}, u32[]{:S(2)}) collective-permute-start(bf16[192,2048]{1,0:T(8,128)(2,1)} %collective-permute-done.6), channel_id=1, source_target_pairs={{0,1},{1,2},{2,3},{3,0},{4,5},{5,6},{6,7},{7,4},{8,9},{9,10},{10,1... | collective-permute-start | bytes 2359304 | tf_op jit(solution)/shard_map/ppermute | solution.py:21
  460.6 157.5 %reduce-scatter.29.cloned.1.call-start = ((), (), s32[]{:S(2)}) async-start(), calls=%async_computation.27 | async-start | bytes 3932160 | tf_op jit(solution)/shard_map/reduce_scatter | solution.py:71
  558.3 132.5 %all-gather.43.cloned.1.call-start = ((), (), s32[]{:S(2)}) async-start(), calls=%async_computation.54 | async-start | bytes 9437184 | tf_op jit(solution)/shard_map/all_gather | solution.py:152
  558.9 181.1 %all-gather.23.cloned.1.call-start = ((), (), s32[]{:S(2)}) async-start(), calls=%async_computation.29 | async-start | bytes 3932160 | tf_op jit(solution)/shard_map/all_gather | solution.py:67
  578.1 218.8 %all-gather.45.cloned.1.call-start = ((), (), s32[]{:S(2)}) async-start(), calls=%async_computation.55 | async-start | bytes 9437184 | tf_op jit(solution)/shard_map/all_gather | solution.py:153
  578.7 304.0 %reduce-scatter.33.cloned.1.call-start = ((), (), s32[]{:S(2)}) async-start(), calls=%async_computation.30 | async-start | bytes 3932160 | tf_op jit(solution)/shard_map/reduce_scatter | solution.py:81
  619.5 265.6 %copy-start.6 = (f32[192,2048]{1,0:T(8,128)}, f32[192,2048]{1,0:T(8,128)S(1)}, u32[]{:S(2)}) copy-start(f32[192,2048]{1,0:T(8,128)S(1)} %get-tuple-element.557) | copy-start | bytes 4718596
  620.3 22.4 collective-permute-start.9
  621.3 36.9 %collective-permute-start.11 = (bf16[192,2048]{1,0:T(8,128)(2,1)S(1)}, bf16[192,2048]{1,0:T(8,128)(2,1)S(1)}, u32[]{:S(2)}, u32[]{:S(2)}) collective-permute-start(bf16[192,2048]{1,0:T(8,128)(2,1)S(1)} %add_convert_fusion.4), channel_id=1, source_target_pairs={{0,3},{1,0},{2,1},{3,2},{4,7},{5,4},{6,5},{7,6},{8,11},{9,8},{10,9... | collective-permute-start | bytes 2359304 | tf_op jit(solution)/shard_map/ppermute | solution.py:24
  642.6 32.4 %collective-permute-start.10 = (bf16[192,2048]{1,0:T(8,128)(2,1)S(1)}, bf16[192,2048]{1,0:T(8,128)(2,1)S(1)}, u32[]{:S(2)}, u32[]{:S(2)}) collective-permute-start(bf16[192,2048]{1,0:T(8,128)(2,1)S(1)} %collective-permute-done.9), channel_id=1, source_target_pairs={{0,1},{1,2},{2,3},{3,0},{4,5},{5,6},{6,7},{7,4},{8,9},{9,10},{10,1... | collective-permute-start | bytes 2359304 | tf_op jit(solution)/shard_map/ppermute | solution.py:21
  822.3 130.2 %all-gather.25.cloned.1.call-start = ((), (), s32[]{:S(2)}) async-start(), calls=%async_computation.31 | async-start | bytes 3932160 | tf_op jit(solution)/shard_map/all_gather | solution.py:67
  888.8 136.8 %reduce-scatter.61.cloned.1.call-start = ((), (), s32[]{:S(2)}) async-start(), calls=%async_computation.56 | async-start | bytes 491520
  1006.2 83.6 %reduce-scatter.35.cloned.1.call-start = ((), (), s32[]{:S(2)}) async-start(), calls=%async_computation.32 | async-start | bytes 3932160 | tf_op jit(solution)/shard_map/reduce_scatter | solution.py:81
  1031.2 130.0 %all-gather.27.cloned.1.call-start = ((), (), s32[]{:S(2)}) async-start(), calls=%async_computation.33 | async-start | bytes 3932160 | tf_op jit(solution)/shard_map/all_gather | solution.py:67
  1097.5 150.1 %reduce-scatter.37.cloned.1.call-start = ((), (), s32[]{:S(2)}) async-start(), calls=%async_computation.34 | async-start | bytes 3932160 | tf_op jit(solution)/shard_map/reduce_scatter | solution.py:81
  1188.6 129.3 %all-gather.29.cloned.1.call-start = ((), (), s32[]{:S(2)}) async-start(), calls=%async_computation.35 | async-start | bytes 3932160 | tf_op jit(solution)/shard_map/all_gather | solution.py:67
  1254.1 131.9 %reduce-scatter.63.cloned.1.call-start = ((), (), s32[]{:S(2)}) async-start(), calls=%async_computation.57 | async-start | bytes 491520
  1366.7 104.0 %reduce-scatter.31.cloned.1.call-start = ((), (), s32[]{:S(2)}) async-start(), calls=%async_computation.28 | async-start | bytes 3932160 | tf_op jit(solution)/shard_map/reduce_scatter | solution.py:71
  1379.9 190.8 %all-reduce.7.cloned.1.call-start = ((), (), s32[]{:S(2)}) async-start(), calls=%async_computation.45 | async-start | bytes 131072 | tf_op jit(solution)/shard_map/psum | solution.py:333
  1380.8 227.4 %reduce-scatter.47.cloned.1.call-start = ((), (), s32[]{:S(2)}) async-start(), calls=%async_computation.40 | async-start | bytes 294912 | tf_op jit(solution)/shard_map/reduce_scatter | solution.py:302
  1383.2 261.8 %reduce-scatter.45.cloned.1.call-start = ((), (), s32[]{:S(2)}) async-start(), calls=%async_computation.39 | async-start | bytes 294912 | tf_op jit(solution)/shard_map/reduce_scatter | solution.py:302
  1389.4 330.3 %reduce-scatter.59.cloned.1.call-start = ((), (), s32[]{:S(2)}) async-start(), calls=%async_computation.47 | async-start | bytes 9437184 | tf_op jit(solution)/shard_map/reduce_scatter | solution.py:311
  1404.0 390.7 %reduce-scatter.57.cloned.1.call-start = ((), (), s32[]{:S(2)}) async-start(), calls=%async_computation.46 | async-start | bytes 9437184 | tf_op jit(solution)/shard_map/reduce_scatter | solution.py:311
  1420.9 436.3 %reduce-scatter.39.cloned.1.call-start = ((), (), s32[]{:S(2)}) async-start(), calls=%async_computation.36 | async-start | bytes 3932160 | tf_op jit(solution)/shard_map/reduce_scatter | solution.py:81
  1428.2 503.8 %reduce-scatter.55.cloned.1.call-start = ((), (), s32[]{:S(2)}) async-start(), calls=%async_computation.44 | async-start | bytes 9437184 | tf_op jit(solution)/shard_map/reduce_scatter | solution.py:308
  1441.0 566.2 %reduce-scatter.53.cloned.1.call-start = ((), (), s32[]{:S(2)}) async-start(), calls=%async_computation.43 | async-start | bytes 9437184 | tf_op jit(solution)/shard_map/reduce_scatter | solution.py:308
  1454.0 597.6 %reduce-scatter.51.cloned.1.call-start = ((), (), s32[]{:S(2)}) async-start(), calls=%async_computation.42 | async-start | bytes 2359296 | tf_op jit(solution)/shard_map/reduce_scatter | solution.py:305
  1460.1 636.4 %reduce-scatter.49.cloned.1.call-start = ((), (), s32[]{:S(2)}) async-start(), calls=%async_computation.41 | async-start | bytes 2359296 | tf_op jit(solution)/shard_map/reduce_scatter | solution.py:305
  1465.2 675.8 %reduce-scatter.43.cloned.1.call-start = ((), (), s32[]{:S(2)}) async-start(), calls=%async_computation.38 | async-start | bytes 2359296 | tf_op jit(solution)/shard_map/reduce_scatter | solution.py:299
  1470.8 101.2 %copy-start.67 = (f32[2048]{0:T(1024)S(1)}, f32[2048]{0:T(1024)}, u32[]{:S(2)}) copy-start(f32[2048]{0:T(1024)} %get-tuple-element.459) | copy-start | bytes 24580
  1470.8 101.2 %copy-start.68 = (f32[2048]{0:T(1024)S(1)}, f32[2048]{0:T(1024)}, u32[]{:S(2)}) copy-start(f32[2048]{0:T(1024)} %get-tuple-element.462) | copy-start | bytes 24580
  1470.8 101.2 %copy-start.71 = (f32[2048]{0:T(1024)S(1)}, f32[2048]{0:T(1024)}, u32[]{:S(2)}) copy-start(f32[2048]{0:T(1024)} %get-tuple-element.461) | copy-start | bytes 24580
  1473.3 16.5 all-to-all-start.2
  1477.0 708.8 %reduce-scatter.41.cloned.1.call-start = ((), (), s32[]{:S(2)}) async-start(), calls=%async_computation.37 | async-start | bytes 2359296 | tf_op jit(solution)/shard_map/reduce_scatter | solution.py:299
  1862.9 458.0 %all-to-all-start.4 = ((bf16[8,24,2048]{2,1,0:T(8,128)(2,1)}), bf16[8,24,2048]{2,1,0:T(8,128)(2,1)S(1)}, u32[]{:S(2)}, u32[]{:S(2)}) async-start(bf16[8,24,2048]{2,1,0:T(8,128)(2,1)} %bitcast.336), calls=%async_computation.12 | async-start | bytes 1572864 | tf_op jit(solution)/shard_map/all_to_all | solution.py:356
  1866.5 451.9 %all-reduce.9.cloned.1.call-start = ((), (), s32[]{:S(2)}) async-start(), calls=%async_computation.58 | async-start | bytes 233472 | tf_op jit(solution)/shard_map/psum | solution.py:333
  2007.2 91.3 %copy-start.69 = (f32[2048]{0:T(1024)S(1)}, f32[2048]{0:T(1024)}, u32[]{:S(2)}) copy-start(f32[2048]{0:T(1024)} %get-tuple-element.465) | copy-start | bytes 24580
  2007.2 91.4 %copy-start.70 = (f32[2048]{0:T(1024)S(1)}, f32[2048]{0:T(1024)}, u32[]{:S(2)}) copy-start(f32[2048]{0:T(1024)} %get-tuple-element.455) | copy-start | bytes 24580
  2007.2 322.9 %copy-start.1 = (bf16[192,2048]{1,0:T(8,128)(2,1)S(1)}, bf16[192,2048]{1,0:T(8,128)(2,1)}, u32[]{:S(2)}) copy-start(bf16[192,2048]{1,0:T(8,128)(2,1)} %param.28) | copy-start | bytes 2359300
  (122 other events, 2817.9 us)
Sparse Core Ops, SparseCore 0:
  10.5 33.2 all-gather.30
  46.3 28.4 all-gather.32
  172.5 60.9 reduce-scatter.24
  235.3 54.3 all-gather.34
  292.0 55.9 all-gather.36
  361.8 60.2 reduce-scatter.26
  424.0 27.9 all-gather.38
  460.7 28.8 all-gather.40
  558.4 59.6 reduce-scatter.28
  619.9 54.4 all-gather.42
  676.4 63.4 all-gather.22
  742.3 54.5 all-gather.44
  822.5 60.2 reduce-scatter.32
  889.0 63.5 all-gather.24
  1006.3 19.3 reduce-scatter.60
  1031.3 58.4 reduce-scatter.34
  1097.6 63.5 all-gather.26
  1188.7 58.8 reduce-scatter.36
  1254.3 63.5 all-gather.28
  1366.8 19.2 reduce-scatter.62
  1388.4 58.5 reduce-scatter.30
  1453.1 117.5 all-reduce.6
  1573.7 34.3 reduce-scatter.46
  1611.3 33.5 reduce-scatter.44
  1648.4 71.2 reduce-scatter.58
  1723.5 71.2 reduce-scatter.56
  1796.9 60.2 reduce-scatter.38
  1860.6 71.3 reduce-scatter.54
  1935.9 71.2 reduce-scatter.52
  2010.3 41.2 reduce-scatter.50
  2055.2 41.2 reduce-scatter.48
  2099.7 41.2 reduce-scatter.42
  2144.5 41.2 reduce-scatter.40
  2193.4 125.0 all-reduce.8
